TPU v7x, 32 devices: a whole 2x2x4 slice. The times are simulated.
32 devices in a mesh: layer: 4 (over y, x), feat: 8 (over z, core).
Axes of the slice: x: 2, y: 2, z: 4, core: 2. Of those that a mesh axis runs over, the one named last changes fastest.
Arguments:
- acts: bfloat16 [4, 256, 8192], P(None, 'layer', 'feat'), may hold values from -6 to 6
- layer_order: int32 [4, 4], P('layer'), may hold values from 0 to 3, each once within a row
- groups: int32 [8192], P('feat'), may hold values from 0 to 63
- group_scale: float32 [4, 64], P('layer'), may hold values from 0.25 to 4
- shrink: float32 [4], P('layer'), may hold values from 0.1 to 0.6
Outputs:
- factor_tiles: float32 [4, 8, 4, 1024, 1024], P('layer', 'feat')
- far_tiles: float32 [4, 8, 512, 1024], P('layer', 'feat')
Inputs may be any that keep to these rules, and one draw needn't show every extreme that they name: Each row of layer_order names every layer once.
All inputs are finite; a program needn't handle non-finite values.
Results may differ from a plain program's by a relative error of at most 0.0003.
Values may be sent and summed in bfloat16 or wider, within the bound.
No kernel may reach another device: no remote copies, remote signals or barrier semaphores. Data moves between devices by JAX's collectives and lax.ppermute only.
A program may use at most 64 MiB of HBM per device.

v0:
```python
import jax
import jax.numpy as jnp
from jax import lax
from jax.sharding import PartitionSpec as P


def shifted(block, axis, distance):
    devices = range(lax.axis_size(axis))
    route = [((i - distance) % len(devices), i) for i in devices]
    return lax.ppermute(block, axis, route)


def product(left, right):
    return lax.dot_general(
        left, right, (((0,), (0,)), ((), ())), preferred_element_type=jnp.float32
    )


def shards(acts, layer_order, groups, group_scale, shrink):
    layers = acts.shape[0]
    pick = (layer_order[0][None, :] == jnp.arange(layers, dtype=jnp.int32)[:, None]).astype(
        jnp.bfloat16
    )
    ordered = jnp.einsum("ds,stc->dtc", pick, acts, preferred_element_type=jnp.float32).astype(
        jnp.bfloat16
    )
    gathered = lax.all_to_all(ordered, "layer", split_axis=0, concat_axis=1, tiled=True)
    panel = gathered[0]
    tokens = panel.shape[0]
    width = panel.shape[1]
    half = lax.axis_size("feat") // 2

    def advance(index, carry):
        moving, stack = carry
        stack = lax.dynamic_update_slice_in_dim(stack, product(panel, moving)[None], index, 0)
        moving = shifted(moving, "feat", -1)
        return (moving, stack)

    start = (panel, jnp.zeros((half, width, width), jnp.float32))
    opposite, grams = lax.fori_loop(0, half, advance, start)
    weight = shrink[0]
    scaled = grams / tokens * (1.0 - weight)
    local_trace = jnp.sum(jnp.diagonal(grams[0]) / tokens)
    mu = lax.psum(local_trace, "feat") / (width * lax.axis_size("feat"))
    members = (
        groups[:, None] == jnp.arange(group_scale.shape[1], dtype=jnp.int32)[None, :]
    ).astype(jnp.float32)
    gains = jnp.dot(members, group_scale[0], precision=lax.Precision.HIGHEST)
    diagonal = weight * mu * gains
    identity = jnp.eye(width, dtype=jnp.float32)
    factor = scaled.at[0].add(diagonal[:, None] * identity)
    lower = lax.axis_index("feat") < half
    rows_half = width // 2
    left = jnp.where(lower, panel[:, :rows_half], opposite[:, rows_half:])
    right = jnp.where(lower, opposite, panel)
    far = product(left, right) / tokens * (1.0 - weight)
    return (factor[None, None], far[None, None])


def solution(mesh):
    placed = (P(None, "layer", "feat"), P("layer", None), P("feat"), P("layer", None), P("layer"))
    return jax.shard_map(
        shards,
        mesh=mesh,
        in_specs=placed,
        out_specs=(P("layer", "feat", None, None, None), P("layer", "feat", None, None)),
        check_vma=False,
    )
```

profile of v0, /device:TPU:0, one launch (start us, length us, event | category | flops | bytes accessed | tf_op | source)
XLA Modules:
  0.0 129.8 jit_solution(15302970972623566115)
XLA Ops:
  0.6 0.0 copy-start
  0.6 1.0 copy-done
  1.7 1.1 convolution_convert_fusion
  2.8 1.0 copy.11
  3.8 5.2 %all-to-all-start = ((bf16[4,64,1024]{2,1,0:T(8,128)(2,1)}), bf16[4,64,1024]{2,1,0:T(8,128)(2,1)S(1)}, u32[]{:S(2)}, u32[]{:S(2)}) async-start(bf16[4,64,1024]{2,1,0:T(8,128)(2,1)} %copy.11), calls=%async_computation | async-start | bytes 1048576 | tf_op jit(solution)/shard_map/all_to_all | solution.py:27
  9.6 1.1 fusion.5
  10.8 6.2 %all-to-all-done = bf16[4,64,1024]{2,1,0:T(8,128)(2,1)S(1)} async-done(((bf16[4,64,1024]{2,1,0:T(8,128)(2,1)}), bf16[4,64,1024]{2,1,0:T(8,128)(2,1)S(1)}, u32[]{:S(2)}, u32[]{:S(2)}) %all-to-all-start) | async-done | bytes 524320 | tf_op jit(solution)/shard_map/all_to_all | solution.py:27
  17.0 40.3 %while.16 = (s32[]{:T(128)}, bf16[256,1024]{1,0:T(8,128)(2,1)S(1)}, f32[4,1024,1024]{2,1,0:T(8,128)}, bf16[256,1024]{1,0:T(8,128)(2,1)S(1)}, s32[]{:T(128)}) while((s32[]{:T(128)}, bf16[256,1024]{1,0:T(8,128)(2,1)S(1)}, f32[4,1024,1024]{2,1,0:T(8,128)}, bf16[256,1024]{1,0:T(8,128)(2,1)S(1)}, s32[]{:T(128)}) %tuple.39), condition=%wide.region_1.0_spmd, body=%wide.region_0.0_spmd.sunk | while | flops 536870912 | bytes 8388721 | solution.py:40
  17.1 2.0 %collective-permute-start = (bf16[256,1024]{1,0:T(8,128)(2,1)S(1)}, bf16[256,1024]{1,0:T(8,128)(2,1)S(1)}, u32[]{:S(2)}, u32[]{:S(2)}) collective-permute-start(bf16[256,1024]{1,0:T(8,128)(2,1)S(1)} %copy.19), channel_id=1, source_target_pairs={{1,0},{2,1},{3,2},{4,3},{5,4},{6,5},{7,6},{0,7},{9,8},{10,9},{11,1... | collective-permute-start | bytes 1572872 | tf_op jit(solution)/shard_map/while/body/eval_jaxpr/ppermute | solution.py:10
  19.1 2.8 %bitcast_dynamic-update-slice_fusion.2 = f32[4,1024,1024]{2,1,0:T(8,128)} fusion(f32[4,1024,1024]{2,1,0:T(8,128)} %get-tuple-element.136, s32[]{:T(128)S(6)} %copy.18, bf16[256,1024]{1,0:T(8,128)(2,1)S(1)} %get-tuple-element.142, bf16[256,1024]{1,0:T(8,128)(2,1)S(1)} %copy.19), kind=kOutput, calls=%fused_computation.1.clone.1 | convolution fusion | flops 536870912 | bytes 5242884 | tf_op jit(solution)/shard_map/while/body/eval_jaxpr/dot_general | solution.py:14
  21.9 3.9 %collective-permute-done = bf16[256,1024]{1,0:T(8,128)(2,1)S(1)} collective-permute-done((bf16[256,1024]{1,0:T(8,128)(2,1)S(1)}, bf16[256,1024]{1,0:T(8,128)(2,1)S(1)}, u32[]{:S(2)}, u32[]{:S(2)}) %collective-permute-start) | collective-permute-done | bytes 524320 | tf_op jit(solution)/shard_map/while/body/eval_jaxpr/ppermute | solution.py:10
  25.8 3.8 %collective-permute-start = (bf16[256,1024]{1,0:T(8,128)(2,1)S(1)}, bf16[256,1024]{1,0:T(8,128)(2,1)S(1)}, u32[]{:S(2)}, u32[]{:S(2)}) collective-permute-start(bf16[256,1024]{1,0:T(8,128)(2,1)S(1)} %copy.19), channel_id=1, source_target_pairs={{1,0},{2,1},{3,2},{4,3},{5,4},{6,5},{7,6},{0,7},{9,8},{10,9},{11,1... | collective-permute-start | bytes 1572872 | tf_op jit(solution)/shard_map/while/body/eval_jaxpr/ppermute | solution.py:10
  29.6 2.8 %bitcast_dynamic-update-slice_fusion.2 = f32[4,1024,1024]{2,1,0:T(8,128)} fusion(f32[4,1024,1024]{2,1,0:T(8,128)} %get-tuple-element.136, s32[]{:T(128)S(6)} %copy.18, bf16[256,1024]{1,0:T(8,128)(2,1)S(1)} %get-tuple-element.142, bf16[256,1024]{1,0:T(8,128)(2,1)S(1)} %copy.19), kind=kOutput, calls=%fused_computation.1.clone.1 | convolution fusion | flops 536870912 | bytes 5242884 | tf_op jit(solution)/shard_map/while/body/eval_jaxpr/dot_general | solution.py:14
  32.4 3.9 %collective-permute-done = bf16[256,1024]{1,0:T(8,128)(2,1)S(1)} collective-permute-done((bf16[256,1024]{1,0:T(8,128)(2,1)S(1)}, bf16[256,1024]{1,0:T(8,128)(2,1)S(1)}, u32[]{:S(2)}, u32[]{:S(2)}) %collective-permute-start) | collective-permute-done | bytes 524320 | tf_op jit(solution)/shard_map/while/body/eval_jaxpr/ppermute | solution.py:10
  36.3 3.8 %collective-permute-start = (bf16[256,1024]{1,0:T(8,128)(2,1)S(1)}, bf16[256,1024]{1,0:T(8,128)(2,1)S(1)}, u32[]{:S(2)}, u32[]{:S(2)}) collective-permute-start(bf16[256,1024]{1,0:T(8,128)(2,1)S(1)} %copy.19), channel_id=1, source_target_pairs={{1,0},{2,1},{3,2},{4,3},{5,4},{6,5},{7,6},{0,7},{9,8},{10,9},{11,1... | collective-permute-start | bytes 1572872 | tf_op jit(solution)/shard_map/while/body/eval_jaxpr/ppermute | solution.py:10
  40.1 2.8 %bitcast_dynamic-update-slice_fusion.2 = f32[4,1024,1024]{2,1,0:T(8,128)} fusion(f32[4,1024,1024]{2,1,0:T(8,128)} %get-tuple-element.136, s32[]{:T(128)S(6)} %copy.18, bf16[256,1024]{1,0:T(8,128)(2,1)S(1)} %get-tuple-element.142, bf16[256,1024]{1,0:T(8,128)(2,1)S(1)} %copy.19), kind=kOutput, calls=%fused_computation.1.clone.1 | convolution fusion | flops 536870912 | bytes 5242884 | tf_op jit(solution)/shard_map/while/body/eval_jaxpr/dot_general | solution.py:14
  42.9 3.9 %collective-permute-done = bf16[256,1024]{1,0:T(8,128)(2,1)S(1)} collective-permute-done((bf16[256,1024]{1,0:T(8,128)(2,1)S(1)}, bf16[256,1024]{1,0:T(8,128)(2,1)S(1)}, u32[]{:S(2)}, u32[]{:S(2)}) %collective-permute-start) | collective-permute-done | bytes 524320 | tf_op jit(solution)/shard_map/while/body/eval_jaxpr/ppermute | solution.py:10
  46.8 3.8 %collective-permute-start = (bf16[256,1024]{1,0:T(8,128)(2,1)S(1)}, bf16[256,1024]{1,0:T(8,128)(2,1)S(1)}, u32[]{:S(2)}, u32[]{:S(2)}) collective-permute-start(bf16[256,1024]{1,0:T(8,128)(2,1)S(1)} %copy.19), channel_id=1, source_target_pairs={{1,0},{2,1},{3,2},{4,3},{5,4},{6,5},{7,6},{0,7},{9,8},{10,9},{11,1... | collective-permute-start | bytes 1572872 | tf_op jit(solution)/shard_map/while/body/eval_jaxpr/ppermute | solution.py:10
  50.6 2.8 %bitcast_dynamic-update-slice_fusion.2 = f32[4,1024,1024]{2,1,0:T(8,128)} fusion(f32[4,1024,1024]{2,1,0:T(8,128)} %get-tuple-element.136, s32[]{:T(128)S(6)} %copy.18, bf16[256,1024]{1,0:T(8,128)(2,1)S(1)} %get-tuple-element.142, bf16[256,1024]{1,0:T(8,128)(2,1)S(1)} %copy.19), kind=kOutput, calls=%fused_computation.1.clone.1 | convolution fusion | flops 536870912 | bytes 5242884 | tf_op jit(solution)/shard_map/while/body/eval_jaxpr/dot_general | solution.py:14
  53.3 3.9 %collective-permute-done = bf16[256,1024]{1,0:T(8,128)(2,1)S(1)} collective-permute-done((bf16[256,1024]{1,0:T(8,128)(2,1)S(1)}, bf16[256,1024]{1,0:T(8,128)(2,1)S(1)}, u32[]{:S(2)}, u32[]{:S(2)}) %collective-permute-start) | collective-permute-done | bytes 524320 | tf_op jit(solution)/shard_map/while/body/eval_jaxpr/ppermute | solution.py:10
  57.3 4.7 %slice_bitcast_fusion = f32[1024,1024]{1,0:T(8,128)} fusion(f32[4,1024,1024]{2,1,0:T(8,128)} %get-tuple-element.94), kind=kLoop, calls=%fused_computation.6 | loop fusion | bytes 8388608 | tf_op jit(solution)/shard_map/squeeze | solution.py:43
  62.0 17.3 %gather_fusion = f32[1024]{0:T(1024)S(1)} fusion(f32[1024,1024]{1,0:T(8,128)} %slice_bitcast_fusion, s32[1024]{0:T(1024)S(1)} %bitcast.36), kind=kCustom, calls=%fused_computation | custom fusion | bytes 16384 | tf_op jit(solution)/shard_map/jit(diagonal)/cond/branch_0_fun/gather | solution.py:43
  79.3 0.6 multiply_reduce_fusion
  79.9 12.2 %broadcast_multiply_fusion = f32[4,1024,1024]{2,1,0:T(8,128)} fusion(f32[4,1024,1024]{2,1,0:T(8,128)} %get-tuple-element.94, f32[]{:T(128)S(6)} %mul.31), kind=kLoop, calls=%fused_computation.2 | loop fusion | flops 4194304 | bytes 33554436 | tf_op jit(solution)/shard_map/mul | solution.py:42
  92.1 12.4 %fusion.15 = f32[1,1,4,1024,1024]{4,3,2,1,0:T(8,128)} fusion(f32[4,1024,1024]{2,1,0:T(8,128)} %get-tuple-element.94, f32[]{:T(128)S(6)} %mul.31), kind=kLoop, calls=%fused_computation.26 | loop fusion | flops 4194304 | bytes 33554436 | tf_op jit(solution)/shard_map/broadcast_in_dim | solution.py:57
  104.5 18.0 %psum.7 = f32[]{:T(128)} all-reduce(f32[]{:T(128)} %multiply_reduce_fusion), channel_id=1, replica_groups=mesh['layer'=4,'feat'=8] {'feat'}, use_global_device_ids=true, to_apply=%region_3.4 | all-reduce | flops 1 | bytes 8 | tf_op jit(solution)/shard_map/psum | solution.py:44
  122.4 1.8 %multiply_bitcast_fusion = f32[1,1,512,1024]{3,2,1,0:T(8,128)} fusion(f32[]{:T(128)S(6)} %mul.31, bf16[256,1024]{1,0:T(8,128)(2,1)S(1)} %get-tuple-element.95, bf16[256,1024]{1,0:T(8,128)(2,1)S(1)} %get-tuple-element.145, pred[]{:T(512)S(6)} %lt.17), kind=kOutput, calls=%fused_computation.8 | convolution fusion | flops 269352960 | bytes 3671552 | tf_op jit(solution)/shard_map/dot_general | solution.py:14
  124.9 4.9 %fusion.1 = f32[1,1,4,1024,1024]{4,3,2,1,0:T(8,128)} fusion(f32[1,1,4,1024,1024]{4,3,2,1,0:T(8,128)} %fusion.15, f32[4,1024,1024]{2,1,0:T(8,128)} %broadcast_multiply_fusion, f32[1024]{0:T(1024)S(1)} %broadcast_multiply_fusion.1), kind=kLoop, calls=%fused_computation.5 | loop fusion | flops 3145728 | bytes 8392704 | tf_op jit(solution)/shard_map/scatter-add | solution.py:51
  (8 shorter events, 0.2 us)
Async XLA Ops:
  0.6 1.0 copy-start
  3.8 13.2 %all-to-all-start = ((bf16[4,64,1024]{2,1,0:T(8,128)(2,1)}), bf16[4,64,1024]{2,1,0:T(8,128)(2,1)S(1)}, u32[]{:S(2)}, u32[]{:S(2)}) async-start(bf16[4,64,1024]{2,1,0:T(8,128)(2,1)} %copy.11), calls=%async_computation | async-start | bytes 1048576 | tf_op jit(solution)/shard_map/all_to_all | solution.py:27
  17.1 8.7 %collective-permute-start = (bf16[256,1024]{1,0:T(8,128)(2,1)S(1)}, bf16[256,1024]{1,0:T(8,128)(2,1)S(1)}, u32[]{:S(2)}, u32[]{:S(2)}) collective-permute-start(bf16[256,1024]{1,0:T(8,128)(2,1)S(1)} %copy.19), channel_id=1, source_target_pairs={{1,0},{2,1},{3,2},{4,3},{5,4},{6,5},{7,6},{0,7},{9,8},{10,9},{11,1... | collective-permute-start | bytes 1572872 | tf_op jit(solution)/shard_map/while/body/eval_jaxpr/ppermute | solution.py:10
  25.8 10.5 %collective-permute-start = (bf16[256,1024]{1,0:T(8,128)(2,1)S(1)}, bf16[256,1024]{1,0:T(8,128)(2,1)S(1)}, u32[]{:S(2)}, u32[]{:S(2)}) collective-permute-start(bf16[256,1024]{1,0:T(8,128)(2,1)S(1)} %copy.19), channel_id=1, source_target_pairs={{1,0},{2,1},{3,2},{4,3},{5,4},{6,5},{7,6},{0,7},{9,8},{10,9},{11,1... | collective-permute-start | bytes 1572872 | tf_op jit(solution)/shard_map/while/body/eval_jaxpr/ppermute | solution.py:10
  36.3 10.5 %collective-permute-start = (bf16[256,1024]{1,0:T(8,128)(2,1)S(1)}, bf16[256,1024]{1,0:T(8,128)(2,1)S(1)}, u32[]{:S(2)}, u32[]{:S(2)}) collective-permute-start(bf16[256,1024]{1,0:T(8,128)(2,1)S(1)} %copy.19), channel_id=1, source_target_pairs={{1,0},{2,1},{3,2},{4,3},{5,4},{6,5},{7,6},{0,7},{9,8},{10,9},{11,1... | collective-permute-start | bytes 1572872 | tf_op jit(solution)/shard_map/while/body/eval_jaxpr/ppermute | solution.py:10
  46.8 10.5 %collective-permute-start = (bf16[256,1024]{1,0:T(8,128)(2,1)S(1)}, bf16[256,1024]{1,0:T(8,128)(2,1)S(1)}, u32[]{:S(2)}, u32[]{:S(2)}) collective-permute-start(bf16[256,1024]{1,0:T(8,128)(2,1)S(1)} %copy.19), channel_id=1, source_target_pairs={{1,0},{2,1},{3,2},{4,3},{5,4},{6,5},{7,6},{0,7},{9,8},{10,9},{11,1... | collective-permute-start | bytes 1572872 | tf_op jit(solution)/shard_map/while/body/eval_jaxpr/ppermute | solution.py:10
where the time goes:
time: 131 us; the launch traced here: 130 us
  other arithmetic  30.1 us (23%)
  local copies, waits for them, and re-layouts  24.2 us (18%)
  waiting for transfers between devices  22 us (17%)
  starting transfers between devices  18.5 us (14%)
  blocking collectives  18 us (14%)
  matrix products  15.1 us (12%)
  between operations  2.03 us (2%)
    psum x1, blocking collectives, shards(): mu = lax.psum(local_trace, 'feat') / (width * lax.axis_size('feat'))  18 us
    gather x1, local copies, waits for them, and re-layouts, shards(): local_trace = jnp.sum(jnp.diagonal(grams[0]) / tokens)  17.3 us
    ppermute x4, waiting for transfers between devices, shifted(): return lax.ppermute(block, axis, route)  15.7 us
    ppermute x4, starting transfers between devices, shifted(): return lax.ppermute(block, axis, route)  13.3 us
    dot_general x5, matrix products, product(): lax.dot_general(left, right, (((0,), (0,)), ((), ())), preferred_element_...  12.8 us
    broadcast_in_dim x1, other arithmetic, shards(): return (factor[None, None], far[None, None])  12.4 us
    mul x1, other arithmetic, shards(): scaled = grams / tokens * (1.0 - weight)  12.2 us
    all_to_all x1, waiting for transfers between devices, shards(): lax.all_to_all(ordered, 'layer', split_axis=0, concat_axis=1, tiled=True)  6.21 us
  transfers between devices with their start and end apart: 5, of which 5 were waited for; matrix products, arithmetic and copies ran while one was open for 9% of the time, Pallas kernels for 0%

commit v1 on v0

--- a/solution.py
+++ b/solution.py
@@ -2,6 +2,29 @@
 import jax.numpy as jnp
 from jax import lax
 from jax.sharding import PartitionSpec as P
+
+
+def split_up(shard, dim, length):
+    shape = shard.shape
+    tiles = shard.reshape(*shape[:dim], length, shape[dim] // length, *shape[dim + 1 :])
+    return jnp.moveaxis(tiles, dim, 0)
+
+
+def joined_along(blocks, dim):
+    lengths = list(blocks.shape[1:])
+    lengths[dim] *= blocks.shape[0]
+    return jnp.moveaxis(blocks, 0, dim).reshape(lengths)
+
+
+def swapped_with_each(shard, axis, split_dim, concat_dim):
+    size, position = (lax.axis_size(axis), lax.axis_index(axis))
+    blocks = split_up(shard, split_dim, size)
+    outs = [blocks[position]]
+    for step in range(1, size):
+        sent = blocks[position ^ step]
+        outs.append(lax.ppermute(sent, axis, [(i, i ^ step) for i in range(size)]))
+    blocks = jnp.stack(outs)[position ^ jnp.arange(size)]
+    return joined_along(blocks, concat_dim)
 
 
 def shifted(block, axis, distance):
@@ -24,7 +47,7 @@
     ordered = jnp.einsum("ds,stc->dtc", pick, acts, preferred_element_type=jnp.float32).astype(
         jnp.bfloat16
     )
-    gathered = lax.all_to_all(ordered, "layer", split_axis=0, concat_axis=1, tiled=True)
+    gathered = swapped_with_each(ordered, "layer", 0, 1)
     panel = gathered[0]
     tokens = panel.shape[0]
     width = panel.shape[1]

time: 131 us -> 136 us (1.038)
  waiting for transfers between devices: 22 us -> 25.3 us
    ppermute x0 -> x3, waiting for transfers between devices: none -> 9.58 us  [swapped_with_each(): outs.append(lax.ppermute(sent, axis, [(i, i ^ step) for i in range(size)]))]
    all_to_all x1 -> x0, waiting for transfers between devices: 6.21 us -> none  [shards(): lax.all_to_all(ordered, 'layer', split_axis=0, concat_axis=1, tiled=True)]
    all_to_all x1 -> x0, starting transfers between devices: 5.19 us -> none  [shards(): lax.all_to_all(ordered, 'layer', split_axis=0, concat_axis=1, tiled=True)]
    ppermute x0 -> x3, starting transfers between devices: none -> 4.63 us  [swapped_with_each(): outs.append(lax.ppermute(sent, axis, [(i, i ^ step) for i in range(size)]))]
  transfers between devices with their start and end apart: 5 -> 7, of which waited for: 5 -> 7; matrix products, arithmetic and copies ran while one was open for 9% -> 9% of each run, Pallas kernels for 0% -> 0%
where the time goes in v1:
time: 136 us; the launch traced here: 135 us
  other arithmetic  30.2 us (22%)
  waiting for transfers between devices  25.3 us (19%)
  local copies, waits for them, and re-layouts  24.9 us (18%)
  starting transfers between devices  19.1 us (14%)
  blocking collectives  17.9 us (13%)
  matrix products  15.1 us (11%)
  between operations  2.06 us (2%)
    psum x1, blocking collectives, shards(): mu = lax.psum(local_trace, 'feat') / (width * lax.axis_size('feat'))  17.9 us
    gather x1, local copies, waits for them, and re-layouts, shards(): local_trace = jnp.sum(jnp.diagonal(grams[0]) / tokens)  17.2 us
    ppermute x4, waiting for transfers between devices, shifted(): return lax.ppermute(block, axis, route)  15.8 us
    ppermute x4, starting transfers between devices, shifted(): return lax.ppermute(block, axis, route)  14.5 us
    dot_general x5, matrix products, product(): lax.dot_general(left, right, (((0,), (0,)), ((), ())), preferred_element_...  12.8 us
    broadcast_in_dim x1, other arithmetic, shards(): return (factor[None, None], far[None, None])  12.4 us
    mul x1, other arithmetic, shards(): scaled = grams / tokens * (1.0 - weight)  12.2 us
    ppermute x3, waiting for transfers between devices, swapped_with_each(): outs.append(lax.ppermute(sent, axis, [(i, i ^ step) for i in range(size)]))  9.58 us
  transfers between devices with their start and end apart: 7, of which 7 were waited for; matrix products, arithmetic and copies ran while one was open for 9% of the time, Pallas kernels for 0%

profile of v1, /device:TPU:0, one launch (start us, length us, event | category | flops | bytes accessed | tf_op | source)
XLA Modules:
  0.0 134.7 jit_solution(7669133510082230624)
XLA Ops:
  0.6 0.0 copy-start
  0.7 1.0 copy-done
  1.7 1.1 convolution_convert_fusion
  2.8 1.1 constant_dynamic-slice_fusion.3
  3.9 4.0 %collective-permute-start.3 = (bf16[1,64,1024]{2,0,1:T(2,128)(2,1)S(1)}, bf16[1,64,1024]{2,0,1:T(2,128)(2,1)S(1)}, u32[]{:S(2)}, u32[]{:S(2)}) collective-permute-start(bf16[1,64,1024]{2,0,1:T(2,128)(2,1)S(1)} %get-tuple-element.105), channel_id=1, source_target_pairs={{0,24},{8,16},{16,8},{24,0},{1,25},{9,17},{17,9},{25,1},{2,26},{10... | collective-permute-start | bytes 393224 | tf_op jit(solution)/shard_map/ppermute | solution.py:25
  7.9 0.5 collective-permute-start.2
  8.4 0.1 collective-permute-start.1
  8.6 1.1 fusion.5
  10.5 4.7 %collective-permute-done.3 = bf16[1,64,1024]{2,0,1:T(2,128)(2,1)S(1)} collective-permute-done((bf16[1,64,1024]{2,0,1:T(2,128)(2,1)S(1)}, bf16[1,64,1024]{2,0,1:T(2,128)(2,1)S(1)}, u32[]{:S(2)}, u32[]{:S(2)}) %collective-permute-start.3) | collective-permute-done | bytes 131104 | tf_op jit(solution)/shard_map/ppermute | solution.py:25
  15.2 4.7 %collective-permute-done.2 = bf16[1,64,1024]{2,0,1:T(2,128)(2,1)S(1)} collective-permute-done((bf16[1,64,1024]{2,0,1:T(2,128)(2,1)S(1)}, bf16[1,64,1024]{2,0,1:T(2,128)(2,1)S(1)}, u32[]{:S(2)}, u32[]{:S(2)}) %collective-permute-start.2) | collective-permute-done | bytes 131104 | tf_op jit(solution)/shard_map/ppermute | solution.py:25
  19.9 0.2 collective-permute-done.1
  20.2 0.1 maximum_bitcast_fusion
  20.3 0.6 gather_fusion
  20.9 41.5 %while.16 = (s32[]{:T(128)}, bf16[256,1024]{1,0:T(8,128)(2,1)S(1)}, f32[4,1024,1024]{2,1,0:T(8,128)}, bf16[256,1024]{1,0:T(8,128)(2,1)S(1)}, s32[]{:T(128)}) while((s32[]{:T(128)}, bf16[256,1024]{1,0:T(8,128)(2,1)S(1)}, f32[4,1024,1024]{2,1,0:T(8,128)}, bf16[256,1024]{1,0:T(8,128)(2,1)S(1)}, s32[]{:T(128)}) %tuple.42), condition=%wide.region_1.0_spmd, body=%wide.region_0.0_spmd.sunk | while | flops 536870912 | bytes 8388721 | solution.py:63
  20.9 3.2 %collective-permute-start = (bf16[256,1024]{1,0:T(8,128)(2,1)S(1)}, bf16[256,1024]{1,0:T(8,128)(2,1)S(1)}, u32[]{:S(2)}, u32[]{:S(2)}) collective-permute-start(bf16[256,1024]{1,0:T(8,128)(2,1)S(1)} %copy.33), channel_id=1, source_target_pairs={{1,0},{2,1},{3,2},{4,3},{5,4},{6,5},{7,6},{0,7},{9,8},{10,9},{11,1... | collective-permute-start | bytes 1572872 | tf_op jit(solution)/shard_map/while/body/eval_jaxpr/ppermute | solution.py:33
  24.2 2.8 %bitcast_dynamic-update-slice_fusion.2 = f32[4,1024,1024]{2,1,0:T(8,128)} fusion(f32[4,1024,1024]{2,1,0:T(8,128)} %get-tuple-element.140, s32[]{:T(128)S(6)} %copy.32, bf16[256,1024]{1,0:T(8,128)(2,1)S(1)} %get-tuple-element.146, bf16[256,1024]{1,0:T(8,128)(2,1)S(1)} %copy.33), kind=kOutput, calls=%fused_computation.2.clone.1 | convolution fusion | flops 536870912 | bytes 5242884 | tf_op jit(solution)/shard_map/while/body/eval_jaxpr/dot_general | solution.py:37
  26.9 3.9 %collective-permute-done = bf16[256,1024]{1,0:T(8,128)(2,1)S(1)} collective-permute-done((bf16[256,1024]{1,0:T(8,128)(2,1)S(1)}, bf16[256,1024]{1,0:T(8,128)(2,1)S(1)}, u32[]{:S(2)}, u32[]{:S(2)}) %collective-permute-start) | collective-permute-done | bytes 524320 | tf_op jit(solution)/shard_map/while/body/eval_jaxpr/ppermute | solution.py:33
  30.9 3.8 %collective-permute-start = (bf16[256,1024]{1,0:T(8,128)(2,1)S(1)}, bf16[256,1024]{1,0:T(8,128)(2,1)S(1)}, u32[]{:S(2)}, u32[]{:S(2)}) collective-permute-start(bf16[256,1024]{1,0:T(8,128)(2,1)S(1)} %copy.33), channel_id=1, source_target_pairs={{1,0},{2,1},{3,2},{4,3},{5,4},{6,5},{7,6},{0,7},{9,8},{10,9},{11,1... | collective-permute-start | bytes 1572872 | tf_op jit(solution)/shard_map/while/body/eval_jaxpr/ppermute | solution.py:33
  34.7 2.8 %bitcast_dynamic-update-slice_fusion.2 = f32[4,1024,1024]{2,1,0:T(8,128)} fusion(f32[4,1024,1024]{2,1,0:T(8,128)} %get-tuple-element.140, s32[]{:T(128)S(6)} %copy.32, bf16[256,1024]{1,0:T(8,128)(2,1)S(1)} %get-tuple-element.146, bf16[256,1024]{1,0:T(8,128)(2,1)S(1)} %copy.33), kind=kOutput, calls=%fused_computation.2.clone.1 | convolution fusion | flops 536870912 | bytes 5242884 | tf_op jit(solution)/shard_map/while/body/eval_jaxpr/dot_general | solution.py:37
  37.4 3.9 %collective-permute-done = bf16[256,1024]{1,0:T(8,128)(2,1)S(1)} collective-permute-done((bf16[256,1024]{1,0:T(8,128)(2,1)S(1)}, bf16[256,1024]{1,0:T(8,128)(2,1)S(1)}, u32[]{:S(2)}, u32[]{:S(2)}) %collective-permute-start) | collective-permute-done | bytes 524320 | tf_op jit(solution)/shard_map/while/body/eval_jaxpr/ppermute | solution.py:33
  41.4 3.8 %collective-permute-start = (bf16[256,1024]{1,0:T(8,128)(2,1)S(1)}, bf16[256,1024]{1,0:T(8,128)(2,1)S(1)}, u32[]{:S(2)}, u32[]{:S(2)}) collective-permute-start(bf16[256,1024]{1,0:T(8,128)(2,1)S(1)} %copy.33), channel_id=1, source_target_pairs={{1,0},{2,1},{3,2},{4,3},{5,4},{6,5},{7,6},{0,7},{9,8},{10,9},{11,1... | collective-permute-start | bytes 1572872 | tf_op jit(solution)/shard_map/while/body/eval_jaxpr/ppermute | solution.py:33
  45.2 2.8 %bitcast_dynamic-update-slice_fusion.2 = f32[4,1024,1024]{2,1,0:T(8,128)} fusion(f32[4,1024,1024]{2,1,0:T(8,128)} %get-tuple-element.140, s32[]{:T(128)S(6)} %copy.32, bf16[256,1024]{1,0:T(8,128)(2,1)S(1)} %get-tuple-element.146, bf16[256,1024]{1,0:T(8,128)(2,1)S(1)} %copy.33), kind=kOutput, calls=%fused_computation.2.clone.1 | convolution fusion | flops 536870912 | bytes 5242884 | tf_op jit(solution)/shard_map/while/body/eval_jaxpr/dot_general | solution.py:37
  47.9 3.9 %collective-permute-done = bf16[256,1024]{1,0:T(8,128)(2,1)S(1)} collective-permute-done((bf16[256,1024]{1,0:T(8,128)(2,1)S(1)}, bf16[256,1024]{1,0:T(8,128)(2,1)S(1)}, u32[]{:S(2)}, u32[]{:S(2)}) %collective-permute-start) | collective-permute-done | bytes 524320 | tf_op jit(solution)/shard_map/while/body/eval_jaxpr/ppermute | solution.py:33
  51.9 3.8 %collective-permute-start = (bf16[256,1024]{1,0:T(8,128)(2,1)S(1)}, bf16[256,1024]{1,0:T(8,128)(2,1)S(1)}, u32[]{:S(2)}, u32[]{:S(2)}) collective-permute-start(bf16[256,1024]{1,0:T(8,128)(2,1)S(1)} %copy.33), channel_id=1, source_target_pairs={{1,0},{2,1},{3,2},{4,3},{5,4},{6,5},{7,6},{0,7},{9,8},{10,9},{11,1... | collective-permute-start | bytes 1572872 | tf_op jit(solution)/shard_map/while/body/eval_jaxpr/ppermute | solution.py:33
  55.7 2.8 %bitcast_dynamic-update-slice_fusion.2 = f32[4,1024,1024]{2,1,0:T(8,128)} fusion(f32[4,1024,1024]{2,1,0:T(8,128)} %get-tuple-element.140, s32[]{:T(128)S(6)} %copy.32, bf16[256,1024]{1,0:T(8,128)(2,1)S(1)} %get-tuple-element.146, bf16[256,1024]{1,0:T(8,128)(2,1)S(1)} %copy.33), kind=kOutput, calls=%fused_computation.2.clone.1 | convolution fusion | flops 536870912 | bytes 5242884 | tf_op jit(solution)/shard_map/while/body/eval_jaxpr/dot_general | solution.py:37
  58.4 3.9 %collective-permute-done = bf16[256,1024]{1,0:T(8,128)(2,1)S(1)} collective-permute-done((bf16[256,1024]{1,0:T(8,128)(2,1)S(1)}, bf16[256,1024]{1,0:T(8,128)(2,1)S(1)}, u32[]{:S(2)}, u32[]{:S(2)}) %collective-permute-start) | collective-permute-done | bytes 524320 | tf_op jit(solution)/shard_map/while/body/eval_jaxpr/ppermute | solution.py:33
  62.4 4.7 %slice_bitcast_fusion = f32[1024,1024]{1,0:T(8,128)} fusion(f32[4,1024,1024]{2,1,0:T(8,128)} %get-tuple-element.94), kind=kLoop, calls=%fused_computation.7 | loop fusion | bytes 8388608 | tf_op jit(solution)/shard_map/squeeze | solution.py:66
  67.1 17.2 %gather_fusion.1 = f32[1024]{0:T(1024)S(1)} fusion(f32[1024,1024]{1,0:T(8,128)} %slice_bitcast_fusion, s32[1024]{0:T(1024)S(1)} %bitcast.52), kind=kCustom, calls=%fused_computation.1 | custom fusion | bytes 16384 | tf_op jit(solution)/shard_map/jit(diagonal)/cond/branch_0_fun/gather | solution.py:66
  84.2 0.6 multiply_reduce_fusion
  84.8 12.2 %broadcast_multiply_fusion = f32[4,1024,1024]{2,1,0:T(8,128)} fusion(f32[4,1024,1024]{2,1,0:T(8,128)} %get-tuple-element.94, f32[]{:T(128)S(6)} %mul.31), kind=kLoop, calls=%fused_computation.3 | loop fusion | flops 4194304 | bytes 33554436 | tf_op jit(solution)/shard_map/mul | solution.py:65
  97.0 12.4 %fusion.16 = f32[1,1,4,1024,1024]{4,3,2,1,0:T(8,128)} fusion(f32[4,1024,1024]{2,1,0:T(8,128)} %get-tuple-element.94, f32[]{:T(128)S(6)} %mul.31), kind=kLoop, calls=%fused_computation.39 | loop fusion | flops 4194304 | bytes 33554436 | tf_op jit(solution)/shard_map/broadcast_in_dim | solution.py:80
  109.4 17.9 %psum.7 = f32[]{:T(128)} all-reduce(f32[]{:T(128)} %multiply_reduce_fusion), channel_id=1, replica_groups=mesh['layer'=4,'feat'=8] {'feat'}, use_global_device_ids=true, to_apply=%region_3.4 | all-reduce | flops 1 | bytes 8 | tf_op jit(solution)/shard_map/psum | solution.py:67
  127.4 1.8 %multiply_bitcast_fusion = f32[1,1,512,1024]{3,2,1,0:T(8,128)} fusion(f32[]{:T(128)S(6)} %mul.31, bf16[256,1024]{1,0:T(8,128)(2,1)S(1)} %get-tuple-element.95, bf16[256,1024]{1,0:T(8,128)(2,1)S(1)} %get-tuple-element.148, pred[]{:T(512)S(6)} %lt.44), kind=kOutput, calls=%fused_computation.9 | convolution fusion | flops 269352960 | bytes 3671552 | tf_op jit(solution)/shard_map/dot_general | solution.py:37
  129.8 4.9 %fusion.1 = f32[1,1,4,1024,1024]{4,3,2,1,0:T(8,128)} fusion(f32[1,1,4,1024,1024]{4,3,2,1,0:T(8,128)} %fusion.16, f32[4,1024,1024]{2,1,0:T(8,128)} %broadcast_multiply_fusion, f32[1024]{0:T(1024)S(1)} %broadcast_multiply_fusion.1), kind=kLoop, calls=%fused_computation.6 | loop fusion | flops 3145728 | bytes 8392704 | tf_op jit(solution)/shard_map/scatter-add | solution.py:74
  (14 shorter events, 0.4 us)
Async XLA Ops:
  0.6 1.0 copy-start
  3.9 11.2 %collective-permute-start.3 = (bf16[1,64,1024]{2,0,1:T(2,128)(2,1)S(1)}, bf16[1,64,1024]{2,0,1:T(2,128)(2,1)S(1)}, u32[]{:S(2)}, u32[]{:S(2)}) collective-permute-start(bf16[1,64,1024]{2,0,1:T(2,128)(2,1)S(1)} %get-tuple-element.105), channel_id=1, source_target_pairs={{0,24},{8,16},{16,8},{24,0},{1,25},{9,17},{17,9},{25,1},{2,26},{10... | collective-permute-start | bytes 393224 | tf_op jit(solution)/shard_map/ppermute | solution.py:25
  7.9 11.9 %collective-permute-start.2 = (bf16[1,64,1024]{2,0,1:T(2,128)(2,1)S(1)}, bf16[1,64,1024]{2,0,1:T(2,128)(2,1)S(1)}, u32[]{:S(2)}, u32[]{:S(2)}) collective-permute-start(bf16[1,64,1024]{2,0,1:T(2,128)(2,1)S(1)} %get-tuple-element.106), channel_id=1, source_target_pairs={{0,16},{8,24},{16,0},{24,8},{1,17},{9,25},{17,1},{25,9},{2,18},{10... | collective-permute-start | bytes 393224 | tf_op jit(solution)/shard_map/ppermute | solution.py:25
  8.4 11.7 %collective-permute-start.1 = (bf16[1,64,1024]{2,0,1:T(2,128)(2,1)S(1)}, bf16[1,64,1024]{2,0,1:T(2,128)(2,1)S(1)}, u32[]{:S(2)}, u32[]{:S(2)}) collective-permute-start(bf16[1,64,1024]{2,0,1:T(2,128)(2,1)S(1)} %get-tuple-element.107), channel_id=1, source_target_pairs={{0,8},{8,0},{16,24},{24,16},{1,9},{9,1},{17,25},{25,17},{2,10},{10... | collective-permute-start | bytes 393224 | tf_op jit(solution)/shard_map/ppermute | solution.py:25
  20.9 9.9 %collective-permute-start = (bf16[256,1024]{1,0:T(8,128)(2,1)S(1)}, bf16[256,1024]{1,0:T(8,128)(2,1)S(1)}, u32[]{:S(2)}, u32[]{:S(2)}) collective-permute-start(bf16[256,1024]{1,0:T(8,128)(2,1)S(1)} %copy.33), channel_id=1, source_target_pairs={{1,0},{2,1},{3,2},{4,3},{5,4},{6,5},{7,6},{0,7},{9,8},{10,9},{11,1... | collective-permute-start | bytes 1572872 | tf_op jit(solution)/shard_map/while/body/eval_jaxpr/ppermute | solution.py:33
  30.9 10.5 %collective-permute-start = (bf16[256,1024]{1,0:T(8,128)(2,1)S(1)}, bf16[256,1024]{1,0:T(8,128)(2,1)S(1)}, u32[]{:S(2)}, u32[]{:S(2)}) collective-permute-start(bf16[256,1024]{1,0:T(8,128)(2,1)S(1)} %copy.33), channel_id=1, source_target_pairs={{1,0},{2,1},{3,2},{4,3},{5,4},{6,5},{7,6},{0,7},{9,8},{10,9},{11,1... | collective-permute-start | bytes 1572872 | tf_op jit(solution)/shard_map/while/body/eval_jaxpr/ppermute | solution.py:33
  41.4 10.5 %collective-permute-start = (bf16[256,1024]{1,0:T(8,128)(2,1)S(1)}, bf16[256,1024]{1,0:T(8,128)(2,1)S(1)}, u32[]{:S(2)}, u32[]{:S(2)}) collective-permute-start(bf16[256,1024]{1,0:T(8,128)(2,1)S(1)} %copy.33), channel_id=1, source_target_pairs={{1,0},{2,1},{3,2},{4,3},{5,4},{6,5},{7,6},{0,7},{9,8},{10,9},{11,1... | collective-permute-start | bytes 1572872 | tf_op jit(solution)/shard_map/while/body/eval_jaxpr/ppermute | solution.py:33
  51.9 10.5 %collective-permute-start = (bf16[256,1024]{1,0:T(8,128)(2,1)S(1)}, bf16[256,1024]{1,0:T(8,128)(2,1)S(1)}, u32[]{:S(2)}, u32[]{:S(2)}) collective-permute-start(bf16[256,1024]{1,0:T(8,128)(2,1)S(1)} %copy.33), channel_id=1, source_target_pairs={{1,0},{2,1},{3,2},{4,3},{5,4},{6,5},{7,6},{0,7},{9,8},{10,9},{11,1... | collective-permute-start | bytes 1572872 | tf_op jit(solution)/shard_map/while/body/eval_jaxpr/ppermute | solution.py:33
